TPU v7x, 256 devices: a whole 4x4x8 slice. The times are simulated.
256 devices in a mesh: slab: 64 (over y, x_lo, z), view: 4 (over x_hi, core).
Axes of the slice: x: 4 (x_hi: 2, x_lo: 2; x = x_hi * 2 + x_lo), y: 4, z: 8, core: 2. Of those that a mesh axis runs over, the one named last changes fastest.
Arguments:
- primal: float32 [5, 256, 32, 128], P(None, 'slab', 'view'), may hold values from -6 to 6
- dual: bfloat16 [64, 256, 128], P('view', 'slab'), may hold values from -6 to 6
- footprints: bfloat16 [8, 128, 128], replicated, may hold values from -0.046875 to 0.046875
- tile_index: int32 [64, 8192, 2], P(None, 'slab'), may hold values from 0 to 3
- footprint_offset: int32 [64, 8192, 2], P(None, 'slab'), may hold values from 0 to 7
- w_first: bfloat16 [3, 3, 3, 32, 6], replicated, may hold values from -0.21875 to 0.21875
- w_middle: bfloat16 [3, 3, 3, 32, 32], replicated, may hold values from -0.21875 to 0.21875
- w_last: bfloat16 [3, 3, 3, 5, 32], replicated, may hold values from -0.5 to 0.5
- cotangent: float32 [5, 256, 32, 128], P(None, 'slab', 'view'), may hold values from -6 to 6
Outputs:
- d_primal: float32 [5, 256, 32, 128], P(None, 'slab', 'view')
- d_dual: float32 [64, 256, 128], P('view', 'slab')
- d_first: float32 [3, 3, 3, 32, 6], replicated
- d_middle: float32 [3, 3, 3, 32, 32], replicated
- d_last: float32 [3, 3, 3, 5, 32], replicated
All inputs are finite; a program needn't handle non-finite values.
Results may differ from a plain program's by a relative error of at most 0.0067.
Values may be sent and summed in bfloat16 or wider, within the bound.
No kernel may reach another device: no remote copies, remote signals or barrier semaphores. Data moves between devices by JAX's collectives and lax.ppermute only.
A program may use at most 64 MiB of HBM per device.

v0:
```python
import math
import jax
import jax.numpy as jnp
from jax import lax
from jax.sharding import PartitionSpec as P


def with_halo(cells, sides, width):
    for axis, dim in sides:
        count = lax.axis_size(axis)
        ends = count - 1
        head = lax.slice_in_dim(cells, 0, width, axis=dim)
        tail = lax.slice_in_dim(cells, cells.shape[dim] - width, cells.shape[dim], axis=dim)
        cells = jnp.concatenate(
            [
                lax.ppermute(tail, axis, [(i, (i + 1) % count) for i in range(ends)]),
                cells,
                lax.ppermute(head, axis, [((i + 1) % count, i) for i in range(ends)]),
            ],
            axis=dim,
        )
    return cells


def silu_slope(value):
    sig = jax.nn.sigmoid(value)
    return sig * (1.0 + value * (1.0 - sig))


def flipped(kernel):
    return kernel[::-1, ::-1, ::-1].transpose(0, 1, 2, 4, 3)


def sideways(padded):
    blank = jnp.zeros(padded.shape[:-1] + (1,), padded.dtype)
    left = jnp.concatenate([blank, padded[..., :-1]], axis=-1)
    right = jnp.concatenate([padded[..., 1:], blank], axis=-1)
    return (left, padded, right)


def rims(field):
    return with_halo(field, (("slab", 1), ("view", 2)), 1)


def convolve(parts, kernel, depth, rows):
    total = None
    for za in range(3):
        for yb in range(3):
            for xc in range(3):
                term = jnp.einsum(
                    "oc,czyx->ozyx",
                    kernel[za, yb, xc],
                    parts[xc][:, za : za + depth, yb : yb + rows, :],
                    preferred_element_type=jnp.float32,
                )
                total = term if total is None else total + term
    return total


def kernel_grad(dout, parts, depth, rows):
    terms = []
    for za in range(3):
        for yb in range(3):
            for xc in range(3):
                terms.append(
                    jnp.einsum(
                        "ozyx,czyx->oc",
                        dout,
                        parts[xc][:, za : za + depth, yb : yb + rows, :],
                        preferred_element_type=jnp.float32,
                    )
                )
    return jnp.stack(terms).reshape(3, 3, 3, dout.shape[0], parts[0].shape[0])


def shards(
    primal, dual, footprints, tile_index, footprint_offset, w_first, w_middle, w_last, cotangent
):
    channels, depth, rows_here, width = primal.shape
    views_here, det_tiles, bins = dual.shape
    all_views = tile_index.shape[0]
    taps = tile_index.shape[2]
    foot_count = footprints.shape[0]
    n_view = lax.axis_size("view")
    full_rows = rows_here * n_view
    x_tiles = width // bins
    view_at = lax.axis_index("view")
    forward_mat = footprints.transpose(1, 0, 2).reshape(bins, foot_count * bins)
    backward_mat = footprints.transpose(2, 0, 1).reshape(bins, foot_count * bins)
    tile_grid = tile_index.reshape(all_views, depth, full_rows, x_tiles, taps)
    foot_grid = footprint_offset.reshape(all_views, depth, full_rows, x_tiles, taps)
    stride = det_tiles * foot_count
    heights = jnp.dot(
        dual.reshape(-1, bins), forward_mat, preferred_element_type=jnp.float32
    ).reshape(-1, bins)
    own_tiles = lax.dynamic_slice_in_dim(tile_grid, view_at * views_here, views_here, 0)
    own_foot = lax.dynamic_slice_in_dim(foot_grid, view_at * views_here, views_here, 0)
    count = rows_here * lax.axis_size("view")

    def strip_add_view(view, total):
        picks = view * stride + own_tiles[view] * foot_count + own_foot[view]
        return total + jnp.take(heights, picks, axis=0).sum(axis=3)

    total = lax.fori_loop(
        0, views_here, strip_add_view, jnp.zeros((depth, count, x_tiles, bins), jnp.float32)
    )
    strips = lax.psum_scatter(
        total.reshape(depth, count, width).transpose(1, 0, 2),
        "view",
        scatter_dimension=0,
        tiled=True,
    )
    back = strips.transpose(1, 0, 2)
    x_zero = jnp.concatenate([primal, back[None]], axis=0).astype(jnp.bfloat16)
    g_low = cotangent.astype(jnp.bfloat16)
    x_parts = sideways(with_halo(x_zero, (("slab", 1), ("view", 2)), 1))
    g_parts = sideways(with_halo(g_low, (("slab", 1), ("view", 2)), 1))
    a_one = convolve(x_parts, w_first, depth, rows_here)
    z_one = jax.nn.silu(a_one).astype(jnp.bfloat16)
    z_one_parts = sideways(rims(z_one))
    a_two = convolve(z_one_parts, w_middle, depth, rows_here)
    z_two = jax.nn.silu(a_two).astype(jnp.bfloat16)
    z_two_parts = sideways(rims(z_two))
    dz_two = convolve(g_parts, flipped(w_last), depth, rows_here)
    d_last = kernel_grad(g_low, z_two_parts, depth, rows_here)
    da_two = (dz_two * silu_slope(a_two)).astype(jnp.bfloat16)
    dz_one = convolve(sideways(rims(da_two)), flipped(w_middle), depth, rows_here)
    d_middle = kernel_grad(da_two, z_one_parts, depth, rows_here)
    da_one = (dz_one * silu_slope(a_one)).astype(jnp.bfloat16)
    dx_zero = convolve(sideways(rims(da_one)), flipped(w_first), depth, rows_here)
    d_first = kernel_grad(da_one, x_parts, depth, rows_here)
    d_primal = cotangent + dx_zero[:channels]
    strip_grad = dx_zero[channels].astype(jnp.bfloat16)
    start_grad = jnp.zeros((views_here * det_tiles, bins), jnp.float32)
    piece = lax.all_gather(strip_grad, "view", axis=1, tiled=True)
    count = piece.shape[1]
    proj = jnp.dot(
        piece.reshape(-1, bins), backward_mat, preferred_element_type=jnp.float32
    ).reshape(-1, bins)
    tile_ids = jnp.arange(depth * count * x_tiles, dtype=jnp.int32).reshape(
        depth, count, x_tiles, 1
    )

    def fold_add_view(view, acc):
        source = tile_ids * foot_count + own_foot[view]
        target = view * det_tiles + own_tiles[view]
        return acc + jax.ops.segment_sum(
            jnp.take(proj, source.reshape(-1), axis=0),
            target.reshape(-1),
            num_segments=views_here * det_tiles,
        )

    d_dual = lax.fori_loop(0, views_here, fold_add_view, start_grad).reshape(
        views_here, det_tiles, bins
    )
    summed = lax.psum((d_first, d_middle, d_last), ("slab", "view"))
    scale = 1.0 / math.sqrt(depth * lax.axis_size("slab") * full_rows * width)
    return (d_primal, d_dual, summed[0] * scale, summed[1] * scale, summed[2] * scale)


def solution(mesh):
    placed = (
        P(None, "slab", "view", None),
        P("view", "slab", None),
        P(),
        P(None, "slab", None),
        P(None, "slab", None),
        P(),
        P(),
        P(),
        P(None, "slab", "view", None),
    )
    return jax.shard_map(
        shards,
        mesh=mesh,
        in_specs=placed,
        out_specs=(P(None, "slab", "view", None), P("view", "slab", None), P(), P(), P()),
        check_vma=False,
    )
```

profile of v0, /device:TPU:1, one launch (start us, length us, event | category | flops | bytes accessed | tf_op | source)
XLA Modules:
  0.0 618.3 jit_solution(12563308730298618970)
XLA Ops:
  7.3 3.5 copy.388
  10.8 2.7 copy.389
  15.7 21.8 %while.30 = (s32[]{:T(128)}, f32[4,32,1,128]{3,2,1,0:T(1,128)S(1)}, s32[16,4,32,1,2]{4,2,1,3,0:T(8,128)S(1)}, s32[16,4,32,1,2]{4,2,1,3,0:T(8,128)S(1)}, f32[512,...) while((s32[]{:T(128)}, f32[4,32,1,128]{3,2,1,0:T(1,128)S(1)}, ...), condition=%wide.region_2.3_spmd.clone, body=%wide.region_0.2_spmd.clone.sunk | while | flops 86788 | bytes 669307 | solution.py:104
  38.3 4.4 collective-permute-start
  47.3 6.5 %collective-permute-start.2 = (bf16[5,6,1,128]{3,2,1,0:T(2,128)(2,1)S(1)}, bf16[5,6,1,128]{3,2,1,0:T(2,128)(2,1)S(1)}, u32[]{:S(2)}, u32[]{:S(2)}) collective-permute-start(bf16[5,6,1,128]{3,2,1,0:T(2,128)(2,1)S(1)} %get-tuple-element.443), channel_id=1, source_target_pairs={{0,1},{1,2},{2,3},{4,5},{5,6},{6,7},{8,9},{9,10},{10,11},{12,13},{... | collective-permute-start | bytes 23048 | tf_op jit(solution)/shard_map/ppermute | solution.py:16
  55.7 4.6 collective-permute-done.3
  68.7 4.5 reduce-scatter.2.cloned.1.call-done
  73.9 3.2 collective-permute-start.4
  81.5 4.7 collective-permute-start.6
  88.3 4.6 collective-permute-done.7
  106.4 3.2 collective-permute-start.8
  112.3 2.8 collective-permute-done.9
  115.2 3.1 collective-permute-start.10
  120.3 4.9 collective-permute-done.11
  158.0 4.8 collective-permute-start.20
  164.1 4.3 collective-permute-start.12
  169.7 240.3 %all-reduce.15.cloned.1.call-done = f32[3,3,3,32,32]{4,3,2,1,0:T(8,128)} async-done(((f32[3,3,3,32,32]{4,3,2,1,0:T(8,128)}), f32[3,3,3,32,32]{4,3,2,1,0:T(8,128)}) %all-reduce.15.cloned.1.call-update) | async-done | bytes 110608 | tf_op jit(solution)/shard_map/psum | solution.py:156
  411.8 5.5 collective-permute-start.22
  419.3 5.1 collective-permute-start.14
  426.6 4.8 collective-permute-done.15
  453.8 80.9 %all-reduce.12 = (f32[3,3,3,32,6]{3,4,2,1,0:T(8,128)S(1)}, f32[3,3,3,5,32]{4,2,3,1,0:T(4,128)S(1)}) all-reduce(f32[3,3,3,32,6]{3,4,2,1,0:T(8,128)} %bitcast.1969, f32[3,3,3,5,32]{4,2,3,1,0:T(4,128)S(1)} %copy.582), channel_id=1, replica_groups=mesh['slab'=64,'view'=4] {'slab','view'}, use_global_device_ids=true, to_apply=%region_7.8 | all-reduce | flops 9504 | bytes 76032 | tf_op jit(solution)/shard_map/psum | solution.py:156
  535.4 3.8 collective-permute-start.18
  542.0 4.1 collective-permute-done.19
  551.5 5.6 all-gather
  557.4 53.1 %while.29 = (s32[]{:T(128)}, f32[64,128]{1,0:T(8,128)S(1)}, s32[16,4,32,1,2]{4,2,1,3,0:T(8,128)S(1)}, s32[16,4,32,1,2]{4,2,1,3,0:T(8,128)S(1)}, f32[1024,128]{1,...) while((s32[]{:T(128)}, f32[64,128]{1,0:T(8,128)S(1)}, ...), condition=%wide.region_6.7_spmd.clone.clone, body=%wide.region_4.6_spmd.clone.clone.sunk | while | flops 70019 | bytes 588653 | solution.py:153
  561.6 2.4 scatter_custom_fusion.6
  565.0 2.4 scatter_custom_fusion.6
  578.2 2.4 scatter_custom_fusion.6
  581.5 2.4 scatter_custom_fusion.6
  584.9 2.4 scatter_custom_fusion.6
  591.5 2.4 scatter_custom_fusion.6
  601.4 2.4 scatter_custom_fusion.6
  (743 shorter events, 171.2 us)
Async XLA Ops:
  7.2 66.0 %reduce-scatter.2.cloned.1.call-start = ((), (), s32[]{:S(2)}) async-start(), calls=%async_computation.1 | async-start | bytes 81920 | tf_op jit(solution)/shard_map/reduce_scatter | solution.py:107
  15.7 28.2 %copy-start.58 = (bf16[3,3,3,5,32]{4,2,3,1,0:T(4,128)(2,1)S(1)}, bf16[3,3,3,5,32]{4,2,3,1,0:T(4,128)(2,1)}, u32[]{:S(2)}) copy-start(bf16[3,3,3,5,32]{4,2,3,1,0:T(4,128)(2,1)} %param.20) | copy-start | bytes 25924
  15.7 28.3 %copy-start.5 = (bf16[3,3,3,32,32]{4,3,2,1,0:T(8,128)(2,1)S(1)}, bf16[3,3,3,32,32]{4,3,2,1,0:T(8,128)(2,1)}, u32[]{:S(2)}) copy-start(bf16[3,3,3,32,32]{4,3,2,1,0:T(8,128)(2,1)} %param.19) | copy-start | bytes 165892
  15.7 28.5 %copy-start.49 = (bf16[3,3,3,32,6]{3,4,2,1,0:T(8,128)(2,1)S(1)}, bf16[3,3,3,32,6]{3,4,2,1,0:T(8,128)(2,1)}, u32[]{:S(2)}) copy-start(bf16[3,3,3,32,6]{3,4,2,1,0:T(8,128)(2,1)} %param.18) | copy-start | bytes 31108
  15.7 29.1 %copy-start.54 = (f32[5,4,8,128]{3,2,1,0:T(8,128)S(1)}, f32[5,4,8,128]{3,2,1,0:T(8,128)}, u32[]{:S(2)}) copy-start(f32[5,4,8,128]{3,2,1,0:T(8,128)} %param.13) | copy-start | bytes 245764
  38.2 371.8 %all-reduce.15.cloned.1.call-start = ((), (), s32[]{:S(2)}) async-start(), calls=%async_computation.2 | async-start | bytes 884736 | tf_op jit(solution)/shard_map/psum | solution.py:156
  38.3 6.6 %collective-permute-start = (bf16[5,1,8,128]{3,2,1,0:T(8,128)(2,1)S(1)}, bf16[5,1,8,128]{3,2,1,0:T(8,128)(2,1)S(1)}, u32[]{:S(2)}, u32[]{:S(2)}) collective-permute-start(bf16[5,1,8,128]{3,2,1,0:T(8,128)(2,1)S(1)} %get-tuple-element.452), channel_id=1, source_target_pairs={{0,4},{4,8},{8,12},{12,16},{16,20},{20,24},{24,28},{28,32},{32,36}... | collective-permute-start | bytes 30728 | tf_op jit(solution)/shard_map/ppermute | solution.py:16
  42.6 4.6 collective-permute-start.1
  44.0 23.4 %copy-start.51 = (bf16[3,3,3,32,5]{3,4,2,1,0:T(8,128)(2,1)}, bf16[3,3,3,32,5]{3,4,2,1,0:T(8,128)(2,1)S(1)}, u32[]{:S(2)}) copy-start(bf16[3,3,3,32,5]{3,4,2,1,0:T(8,128)(2,1)S(1)} %reverse_bitcast_fusion.2) | copy-start | bytes 25924
  47.3 8.4 %collective-permute-start.2 = (bf16[5,6,1,128]{3,2,1,0:T(2,128)(2,1)S(1)}, bf16[5,6,1,128]{3,2,1,0:T(2,128)(2,1)S(1)}, u32[]{:S(2)}, u32[]{:S(2)}) collective-permute-start(bf16[5,6,1,128]{3,2,1,0:T(2,128)(2,1)S(1)} %get-tuple-element.443), channel_id=1, source_target_pairs={{0,1},{1,2},{2,3},{4,5},{5,6},{6,7},{8,9},{9,10},{10,11},{12,13},{... | collective-permute-start | bytes 23048 | tf_op jit(solution)/shard_map/ppermute | solution.py:16
  53.7 6.6 %collective-permute-start.3 = (bf16[5,6,1,128]{3,2,1,0:T(2,128)(2,1)S(1)}, bf16[5,6,1,128]{3,2,1,0:T(2,128)(2,1)S(1)}, u32[]{:S(2)}, u32[]{:S(2)}) collective-permute-start(bf16[5,6,1,128]{3,2,1,0:T(2,128)(2,1)S(1)} %get-tuple-element.444), channel_id=1, source_target_pairs={{1,0},{2,1},{3,2},{5,4},{6,5},{7,6},{9,8},{10,9},{11,10},{13,12},{... | collective-permute-start | bytes 23048 | tf_op jit(solution)/shard_map/ppermute | solution.py:18
  73.9 5.5 collective-permute-start.4
  77.1 4.4 collective-permute-start.5
  81.5 6.7 %collective-permute-start.6 = (bf16[6,6,1,128]{3,2,1,0:T(2,128)(2,1)S(1)}, bf16[6,6,1,128]{3,2,1,0:T(2,128)(2,1)S(1)}, u32[]{:S(2)}, u32[]{:S(2)}) collective-permute-start(bf16[6,6,1,128]{3,2,1,0:T(2,128)(2,1)S(1)} %get-tuple-element.440), channel_id=1, source_target_pairs={{0,1},{1,2},{2,3},{4,5},{5,6},{6,7},{8,9},{9,10},{10,11},{12,13},{... | collective-permute-start | bytes 27656 | tf_op jit(solution)/shard_map/ppermute | solution.py:16
  86.3 6.6 %collective-permute-start.7 = (bf16[6,6,1,128]{3,2,1,0:T(2,128)(2,1)S(1)}, bf16[6,6,1,128]{3,2,1,0:T(2,128)(2,1)S(1)}, u32[]{:S(2)}, u32[]{:S(2)}) collective-permute-start(bf16[6,6,1,128]{3,2,1,0:T(2,128)(2,1)S(1)} %get-tuple-element.439), channel_id=1, source_target_pairs={{1,0},{2,1},{3,2},{5,4},{6,5},{7,6},{9,8},{10,9},{11,10},{13,12},{... | collective-permute-start | bytes 27656 | tf_op jit(solution)/shard_map/ppermute | solution.py:18
  106.4 5.9 collective-permute-start.8
  109.6 5.6 collective-permute-start.9
  115.2 5.1 collective-permute-start.10
  118.3 6.9 %collective-permute-start.11 = (bf16[32,6,1,128]{3,0,2,1:T(8,128)(2,1)S(1)}, bf16[32,6,1,128]{3,0,2,1:T(8,128)(2,1)S(1)}, u32[]{:S(2)}, u32[]{:S(2)}) collective-permute-start(bf16[32,6,1,128]{3,0,2,1:T(8,128)(2,1)S(1)} %get-tuple-element.372), channel_id=1, source_target_pairs={{1,0},{2,1},{3,2},{5,4},{6,5},{7,6},{9,8},{10,9},{11,10},{13,12},{... | collective-permute-start | bytes 147464 | tf_op jit(solution)/shard_map/ppermute | solution.py:18
  158.0 253.8 %collective-permute-start.20 = (bf16[32,1,8,128]{3,0,2,1:T(8,128)(2,1)}, bf16[32,1,8,128]{3,0,2,1:T(8,128)(2,1)S(1)}, u32[]{:S(2)}, u32[]{:S(2)}) collective-permute-start(bf16[32,1,8,128]{3,0,2,1:T(8,128)(2,1)} %get-tuple-element.375), channel_id=1, source_target_pairs={{0,4},{4,8},{8,12},{12,16},{16,20},{20,24},{24,28},{28,32},{32,36}... | collective-permute-start | bytes 196616 | tf_op jit(solution)/shard_map/ppermute | solution.py:16
  162.8 249.0 %collective-permute-start.21 = (bf16[32,1,8,128]{3,0,2,1:T(8,128)(2,1)}, bf16[32,1,8,128]{3,0,2,1:T(8,128)(2,1)S(1)}, u32[]{:S(2)}, u32[]{:S(2)}) collective-permute-start(bf16[32,1,8,128]{3,0,2,1:T(8,128)(2,1)} %get-tuple-element.376), channel_id=1, source_target_pairs={{4,0},{8,4},{12,8},{16,12},{20,16},{24,20},{28,24},{32,28},{36,32}... | collective-permute-start | bytes 196616 | tf_op jit(solution)/shard_map/ppermute | solution.py:18
  164.1 255.2 %collective-permute-start.12 = (bf16[32,1,8,128]{3,0,2,1:T(8,128)(2,1)}, bf16[32,1,8,128]{3,0,2,1:T(8,128)(2,1)S(1)}, u32[]{:S(2)}, u32[]{:S(2)}) collective-permute-start(bf16[32,1,8,128]{3,0,2,1:T(8,128)(2,1)} %get-tuple-element.379), channel_id=1, source_target_pairs={{0,4},{4,8},{8,12},{12,16},{16,20},{20,24},{24,28},{28,32},{32,36}... | collective-permute-start | bytes 196616 | tf_op jit(solution)/shard_map/ppermute | solution.py:16
  168.4 250.9 %collective-permute-start.13 = (bf16[32,1,8,128]{3,0,2,1:T(8,128)(2,1)}, bf16[32,1,8,128]{3,0,2,1:T(8,128)(2,1)S(1)}, u32[]{:S(2)}, u32[]{:S(2)}) collective-permute-start(bf16[32,1,8,128]{3,0,2,1:T(8,128)(2,1)} %get-tuple-element.380), channel_id=1, source_target_pairs={{4,0},{8,4},{12,8},{16,12},{20,16},{24,20},{28,24},{32,28},{36,32}... | collective-permute-start | bytes 196616 | tf_op jit(solution)/shard_map/ppermute | solution.py:18
  411.8 27.3 %collective-permute-start.22 = (bf16[32,6,1,128]{3,0,2,1:T(8,128)(2,1)S(1)}, bf16[32,6,1,128]{3,0,2,1:T(8,128)(2,1)S(1)}, u32[]{:S(2)}, u32[]{:S(2)}) collective-permute-start(bf16[32,6,1,128]{3,0,2,1:T(8,128)(2,1)S(1)} %get-tuple-element.361), channel_id=1, source_target_pairs={{0,1},{1,2},{2,3},{4,5},{5,6},{6,7},{8,9},{9,10},{10,11},{12,13},{... | collective-permute-start | bytes 147464 | tf_op jit(solution)/shard_map/ppermute | solution.py:16
  417.3 21.8 %collective-permute-start.23 = (bf16[32,6,1,128]{3,0,2,1:T(8,128)(2,1)S(1)}, bf16[32,6,1,128]{3,0,2,1:T(8,128)(2,1)S(1)}, u32[]{:S(2)}, u32[]{:S(2)}) collective-permute-start(bf16[32,6,1,128]{3,0,2,1:T(8,128)(2,1)S(1)} %get-tuple-element.362), channel_id=1, source_target_pairs={{1,0},{2,1},{3,2},{5,4},{6,5},{7,6},{9,8},{10,9},{11,10},{13,12},{... | collective-permute-start | bytes 147464 | tf_op jit(solution)/shard_map/ppermute | solution.py:18
  419.3 7.3 %collective-permute-start.14 = (bf16[32,6,1,128]{3,0,2,1:T(8,128)(2,1)S(1)}, bf16[32,6,1,128]{3,0,2,1:T(8,128)(2,1)S(1)}, u32[]{:S(2)}, u32[]{:S(2)}) collective-permute-start(bf16[32,6,1,128]{3,0,2,1:T(8,128)(2,1)S(1)} %get-tuple-element.367), channel_id=1, source_target_pairs={{0,1},{1,2},{2,3},{4,5},{5,6},{6,7},{8,9},{9,10},{10,11},{12,13},{... | collective-permute-start | bytes 147464 | tf_op jit(solution)/shard_map/ppermute | solution.py:16
  424.5 6.9 %collective-permute-start.15 = (bf16[32,6,1,128]{3,0,2,1:T(8,128)(2,1)S(1)}, bf16[32,6,1,128]{3,0,2,1:T(8,128)(2,1)S(1)}, u32[]{:S(2)}, u32[]{:S(2)}) collective-permute-start(bf16[32,6,1,128]{3,0,2,1:T(8,128)(2,1)S(1)} %get-tuple-element.368), channel_id=1, source_target_pairs={{1,0},{2,1},{3,2},{5,4},{6,5},{7,6},{9,8},{10,9},{11,10},{13,12},{... | collective-permute-start | bytes 147464 | tf_op jit(solution)/shard_map/ppermute | solution.py:18
  450.9 84.4 %collective-permute-start.16 = (bf16[32,1,8,128]{3,0,2,1:T(8,128)(2,1)}, bf16[32,1,8,128]{3,0,2,1:T(8,128)(2,1)S(1)}, u32[]{:S(2)}, u32[]{:S(2)}) collective-permute-start(bf16[32,1,8,128]{3,0,2,1:T(8,128)(2,1)} %get-tuple-element.377), channel_id=1, source_target_pairs={{0,4},{4,8},{8,12},{12,16},{16,20},{20,24},{24,28},{28,32},{32,36}... | collective-permute-start | bytes 196616 | tf_op jit(solution)/shard_map/ppermute | solution.py:16
  452.3 83.0 %collective-permute-start.17 = (bf16[32,1,8,128]{3,0,2,1:T(8,128)(2,1)}, bf16[32,1,8,128]{3,0,2,1:T(8,128)(2,1)S(1)}, u32[]{:S(2)}, u32[]{:S(2)}) collective-permute-start(bf16[32,1,8,128]{3,0,2,1:T(8,128)(2,1)} %get-tuple-element.378), channel_id=1, source_target_pairs={{4,0},{8,4},{12,8},{16,12},{20,16},{24,20},{28,24},{32,28},{36,32}... | collective-permute-start | bytes 196616 | tf_op jit(solution)/shard_map/ppermute | solution.py:18
  535.4 6.6 %collective-permute-start.18 = (bf16[32,6,1,128]{3,0,2,1:T(8,128)(2,1)S(1)}, bf16[32,6,1,128]{3,0,2,1:T(8,128)(2,1)S(1)}, u32[]{:S(2)}, u32[]{:S(2)}) collective-permute-start(bf16[32,6,1,128]{3,0,2,1:T(8,128)(2,1)S(1)} %get-tuple-element.363), channel_id=1, source_target_pairs={{0,1},{1,2},{2,3},{4,5},{5,6},{6,7},{8,9},{9,10},{10,11},{12,13},{... | collective-permute-start | bytes 147464 | tf_op jit(solution)/shard_map/ppermute | solution.py:16
  539.2 6.9 %collective-permute-start.19 = (bf16[32,6,1,128]{3,0,2,1:T(8,128)(2,1)S(1)}, bf16[32,6,1,128]{3,0,2,1:T(8,128)(2,1)S(1)}, u32[]{:S(2)}, u32[]{:S(2)}) collective-permute-start(bf16[32,6,1,128]{3,0,2,1:T(8,128)(2,1)S(1)} %get-tuple-element.364), channel_id=1, source_target_pairs={{1,0},{2,1},{3,2},{5,4},{6,5},{7,6},{9,8},{10,9},{11,10},{13,12},{... | collective-permute-start | bytes 147464 | tf_op jit(solution)/shard_map/ppermute | solution.py:18
  557.1 54.1 %copy-start.1 = (bf16[16,4,128]{2,1,0:T(4,128)(2,1)S(1)}, bf16[16,4,128]{2,1,0:T(4,128)(2,1)}, u32[]{:S(2)}) copy-start(bf16[16,4,128]{2,1,0:T(4,128)(2,1)} %param.14) | copy-start | bytes 49156
  (56 other events, 319.5 us)
Sparse Core Ops, SparseCore 0:
  38.3 34.8 reduce-scatter.1
  157.4 252.5 all-reduce.14
where the time goes:
time: 628 us; the launch traced here: 618 us
  waiting for transfers between devices  275 us (44%)
  blocking collectives  86.5 us (14%)
  matrix products  72.4 us (12%)
  starting transfers between devices  70.2 us (11%)
  other arithmetic  51.7 us (8%)
  local copies, waits for them, and re-layouts  44 us (7%)
  between operations  16.3 us (3%)
    psum x1, waiting for transfers between devices, shards(): summed = lax.psum((d_first, d_middle, d_last), ('slab', 'view'))  240 us
    psum x1, blocking collectives, shards(): summed = lax.psum((d_first, d_middle, d_last), ('slab', 'view'))  80.9 us
    ppermute x12, starting transfers between devices, with_halo(): lax.ppermute(tail, axis, [(i, (i + 1) % count) for i in range(ends)])  50 us
    dot_general x135, matrix products, convolve(): jnp.einsum('oc,czyx->ozyx', kernel[za, yb, xc], parts[xc][:, za:za + dept...  40 us
    scatter-add x16, other arithmetic, fold_add_view(): jax.ops.segment_sum(jnp.take(proj, source.reshape(-1), axis=0), target.re...  38.8 us
    dot_general x81, matrix products, kernel_grad(): jnp.einsum('ozyx,czyx->oc', dout, parts[xc][:, za:za + depth, yb:yb + row...  31.9 us
    ppermute x12, waiting for transfers between devices, with_halo(): lax.ppermute(head, axis, [((i + 1) % count, i) for i in range(ends)])  30.4 us
    ppermute x12, starting transfers between devices, with_halo(): lax.ppermute(head, axis, [((i + 1) % count, i) for i in range(ends)])  20.1 us
  transfers between devices with their start and end apart: 26, of which 10 were waited for; matrix products, arithmetic and copies ran while one was open for 4% of the time, Pallas kernels for 0%

commit v1 on v0

--- a/solution.py
+++ b/solution.py
@@ -153,7 +153,7 @@
     d_dual = lax.fori_loop(0, views_here, fold_add_view, start_grad).reshape(
         views_here, det_tiles, bins
     )
-    summed = lax.psum((d_first, d_middle, d_last), ("slab", "view"))
+    summed = lax.psum(lax.psum((d_first, d_middle, d_last), "slab"), "view")
     scale = 1.0 / math.sqrt(depth * lax.axis_size("slab") * full_rows * width)
     return (d_primal, d_dual, summed[0] * scale, summed[1] * scale, summed[2] * scale)
 

time: 628 us -> 1220 us (1.94)
  waiting for transfers between devices: 275 us -> 564 us
  blocking collectives: 86.5 us -> 371 us
  matrix products: 72.4 us -> 87.1 us
    psum x1 -> x2, waiting for transfers between devices: 240 us -> 530 us  [shards(): summed = lax.psum(lax.psum((d_first, d_middle, d_last), 'slab'), 'view')]
    psum x1 -> x2, blocking collectives: 80.9 us -> 365 us  [shards(): summed = lax.psum(lax.psum((d_first, d_middle, d_last), 'slab'), 'view')]
    dot_general x81, matrix products: 31.9 us -> 48 us  [kernel_grad(): jnp.einsum('ozyx,czyx->oc', dout, parts[xc][:, za:za + depth, yb:yb + row...]
  transfers between devices with their start and end apart: 26 -> 27, of which waited for: 10 -> 10; matrix products, arithmetic and copies ran while one was open for 4% -> 5% of each run, Pallas kernels for 0% -> 0%
where the time goes in v1:
time: 1220 us; the launch traced here: 1210 us
  waiting for transfers between devices  564 us (46%)
  blocking collectives  371 us (30%)
  matrix products  87.1 us (7%)
  starting transfers between devices  69.1 us (6%)
  other arithmetic  57.1 us (5%)
  local copies, waits for them, and re-layouts  44 us (4%)
  between operations  16.1 us (1%)
    psum x2, waiting for transfers between devices, shards(): summed = lax.psum(lax.psum((d_first, d_middle, d_last), 'slab'), 'view')  530 us
    psum x2, blocking collectives, shards(): summed = lax.psum(lax.psum((d_first, d_middle, d_last), 'slab'), 'view')  365 us
    ppermute x12, starting transfers between devices, with_halo(): lax.ppermute(tail, axis, [(i, (i + 1) % count) for i in range(ends)])  48.3 us
    dot_general x81, matrix products, kernel_grad(): jnp.einsum('ozyx,czyx->oc', dout, parts[xc][:, za:za + depth, yb:yb + row...  48 us
    scatter-add x16, other arithmetic, fold_add_view(): jax.ops.segment_sum(jnp.take(proj, source.reshape(-1), axis=0), target.re...  38.8 us
    dot_general x135, matrix products, convolve(): jnp.einsum('oc,czyx->ozyx', kernel[za, yb, xc], parts[xc][:, za:za + dept...  38.6 us
    ppermute x12, waiting for transfers between devices, with_halo(): lax.ppermute(head, axis, [((i + 1) % count, i) for i in range(ends)])  28.5 us
  transfers between devices with their start and end apart: 27, of which 10 were waited for; matrix products, arithmetic and copies ran while one was open for 5% of the time, Pallas kernels for 0%

profile of v1, /device:TPU:1, one launch (start us, length us, event | category | flops | bytes accessed | tf_op | source)
XLA Modules:
  0.0 1209.4 jit_solution(12824381290203328585)
XLA Ops:
  7.3 3.5 copy.388
  10.8 2.7 copy.389
  15.8 21.8 %while.30 = (s32[]{:T(128)}, f32[4,32,1,128]{3,2,1,0:T(1,128)S(1)}, s32[16,4,32,1,2]{4,2,1,3,0:T(8,128)S(1)}, s32[16,4,32,1,2]{4,2,1,3,0:T(8,128)S(1)}, f32[512,...) while((s32[]{:T(128)}, f32[4,32,1,128]{3,2,1,0:T(1,128)S(1)}, ...), condition=%wide.region_2.3_spmd.clone, body=%wide.region_0.2_spmd.clone.sunk | while | flops 86788 | bytes 669307 | solution.py:104
  38.3 4.4 collective-permute-start
  47.3 6.5 collective-permute-start.2
  55.7 4.6 collective-permute-done.3
  68.0 5.2 reduce-scatter.2.cloned.1.call-done
  73.9 3.2 collective-permute-start.4
  78.7 2.8 collective-permute-done.5
  81.6 4.7 collective-permute-start.6
  88.3 4.6 collective-permute-done.7
  106.4 3.2 collective-permute-start.8
  112.4 2.8 collective-permute-done.9
  115.2 3.1 collective-permute-start.10
  120.3 4.9 collective-permute-done.11
  154.0 4.8 collective-permute-start.20
  164.2 4.3 collective-permute-start.12
  170.4 2.4 collective-permute-start.22
  172.9 2.5 collective-permute-start.23
  176.1 4.6 collective-permute-start.14
  183.6 529.7 %all-reduce.17.cloned.1.call-done = f32[3,3,3,32,32]{4,3,2,1,0:T(8,128)} async-done(((f32[3,3,3,32,32]{4,3,2,1,0:T(8,128)}), f32[3,3,3,32,32]{4,3,2,1,0:T(8,128)}) %all-reduce.17.cloned.1.call-update) | async-done | bytes 110608 | tf_op jit(solution)/shard_map/psum | solution.py:156
  752.3 252.6 %all-reduce.12 = (f32[3,3,3,32,6]{3,4,2,1,0:T(8,128)S(1)}, f32[3,3,3,5,32]{4,2,3,1,0:T(4,128)S(1)}) all-reduce(f32[3,3,3,32,6]{3,4,2,1,0:T(8,128)} %bitcast.559, f32[3,3,3,5,32]{4,2,3,1,0:T(4,128)S(1)} %copy.582), channel_id=1, replica_groups=mesh['slab'=64,'view'=4] {'slab'}, use_global_device_ids=true, to_apply=%region_7.8 | all-reduce | flops 9504 | bytes 76032 | tf_op jit(solution)/shard_map/psum | solution.py:156
  1004.9 112.4 %all-reduce.13 = (f32[3,3,3,32,6]{3,4,2,1,0:T(8,128)S(1)}, f32[3,3,3,5,32]{4,2,3,1,0:T(4,128)S(1)}) all-reduce(f32[3,3,3,32,6]{3,4,2,1,0:T(8,128)S(1)} %get-tuple-element.299, f32[3,3,3,5,32]{4,2,3,1,0:T(4,128)S(1)} %get-tuple-element.300), channel_id=1, replica_groups=mesh['slab'=64,'view'=4] {'view'}, use_global_device_ids=true, to_apply=%region_8.9 | all-reduce | flops 9504 | bytes 76032 | tf_op jit(solution)/shard_map/psum | solution.py:156
  1121.4 3.4 collective-permute-done.17
  1124.8 5.9 collective-permute-start.18
  1134.7 2.9 collective-permute-done.19
  1143.0 5.6 all-gather
  1148.9 53.1 %while.29 = (s32[]{:T(128)}, f32[64,128]{1,0:T(8,128)S(1)}, s32[16,4,32,1,2]{4,2,1,3,0:T(8,128)S(1)}, s32[16,4,32,1,2]{4,2,1,3,0:T(8,128)S(1)}, f32[1024,128]{1,...) while((s32[]{:T(128)}, f32[64,128]{1,0:T(8,128)S(1)}, ...), condition=%wide.region_6.7_spmd.clone.clone, body=%wide.region_4.6_spmd.clone.clone.sunk | while | flops 70019 | bytes 588653 | solution.py:153
  1153.1 2.4 scatter_custom_fusion.6
  1156.5 2.4 scatter_custom_fusion.6
  1169.7 2.4 scatter_custom_fusion.6
  1176.3 2.4 scatter_custom_fusion.6
  (751 shorter events, 194.4 us)
Async XLA Ops:
  7.2 66.0 %reduce-scatter.2.cloned.1.call-start = ((), (), s32[]{:S(2)}) async-start(), calls=%async_computation.1 | async-start | bytes 81920 | tf_op jit(solution)/shard_map/reduce_scatter | solution.py:107
  15.8 29.1 %copy-start.55 = (f32[5,4,8,128]{3,2,1,0:T(8,128)S(1)}, f32[5,4,8,128]{3,2,1,0:T(8,128)}, u32[]{:S(2)}) copy-start(f32[5,4,8,128]{3,2,1,0:T(8,128)} %param.13) | copy-start | bytes 245764
  38.2 675.1 %all-reduce.17.cloned.1.call-start = ((), (), s32[]{:S(2)}) async-start(), calls=%async_computation.2 | async-start | bytes 884736 | tf_op jit(solution)/shard_map/psum | solution.py:156
  38.3 6.6 collective-permute-start
  42.7 4.6 collective-permute-start.1
  44.0 34.4 %copy-start.53 = (bf16[3,3,3,32,5]{3,4,2,1,0:T(8,128)(2,1)}, bf16[3,3,3,32,5]{3,4,2,1,0:T(8,128)(2,1)S(1)}, u32[]{:S(2)}) copy-start(bf16[3,3,3,32,5]{3,4,2,1,0:T(8,128)(2,1)S(1)} %reverse_bitcast_fusion.2) | copy-start | bytes 25924
  47.3 8.4 collective-permute-start.2
  53.8 6.6 collective-permute-start.3
  73.9 4.8 collective-permute-start.4
  77.1 4.4 collective-permute-start.5
  81.6 6.7 collective-permute-start.6
  86.3 6.6 collective-permute-start.7
  106.4 5.9 collective-permute-start.8
  109.6 5.6 collective-permute-start.9
  115.2 5.1 collective-permute-start.10
  118.3 6.9 collective-permute-start.11
  154.0 15.7 %collective-permute-start.20 = (bf16[32,1,8,128]{3,0,2,1:T(8,128)(2,1)}, bf16[32,1,8,128]{3,0,2,1:T(8,128)(2,1)S(1)}, u32[]{:S(2)}, u32[]{:S(2)}) collective-permute-start(bf16[32,1,8,128]{3,0,2,1:T(8,128)(2,1)} %get-tuple-element.377), channel_id=1, source_target_pairs={{0,4},{4,8},{8,12},{12,16},{16,20},{20,24},{24,28},{28,32},{32,36}... | collective-permute-start | bytes 196616 | tf_op jit(solution)/shard_map/ppermute | solution.py:16
  158.9 10.9 collective-permute-start.21
  164.1 968.7 %all-reduce.19.cloned.1.call-start = ((), (), s32[]{:S(2)}) async-start(), calls=%async_computation.3 | async-start | bytes 884736 | tf_op jit(solution)/shard_map/psum | solution.py:156
  164.2 11.2 collective-permute-start.12
  168.5 6.9 collective-permute-start.13
  170.4 552.9 %collective-permute-start.22 = (bf16[32,6,1,128]{3,0,2,1:T(8,128)(2,1)}, bf16[32,6,1,128]{3,0,2,1:T(8,128)(2,1)}, u32[]{:S(2)}, u32[]{:S(2)}) collective-permute-start(bf16[32,6,1,128]{3,0,2,1:T(8,128)(2,1)} %get-tuple-element.363), channel_id=1, source_target_pairs={{0,1},{1,2},{2,3},{4,5},{5,6},{6,7},{8,9},{9,10},{10,11},{12,13},{... | collective-permute-start | bytes 147464 | tf_op jit(solution)/shard_map/ppermute | solution.py:16
  172.9 550.5 %collective-permute-start.23 = (bf16[32,6,1,128]{3,0,2,1:T(8,128)(2,1)}, bf16[32,6,1,128]{3,0,2,1:T(8,128)(2,1)}, u32[]{:S(2)}, u32[]{:S(2)}) collective-permute-start(bf16[32,6,1,128]{3,0,2,1:T(8,128)(2,1)} %get-tuple-element.364), channel_id=1, source_target_pairs={{1,0},{2,1},{3,2},{5,4},{6,5},{7,6},{9,8},{10,9},{11,10},{13,12},{... | collective-permute-start | bytes 147464 | tf_op jit(solution)/shard_map/ppermute | solution.py:18
  176.1 537.3 %collective-permute-start.14 = (bf16[32,6,1,128]{3,0,2,1:T(8,128)(2,1)}, bf16[32,6,1,128]{3,0,2,1:T(8,128)(2,1)}, u32[]{:S(2)}, u32[]{:S(2)}) collective-permute-start(bf16[32,6,1,128]{3,0,2,1:T(8,128)(2,1)} %get-tuple-element.369), channel_id=1, source_target_pairs={{0,1},{1,2},{2,3},{4,5},{5,6},{6,7},{8,9},{9,10},{10,11},{12,13},{... | collective-permute-start | bytes 147464 | tf_op jit(solution)/shard_map/ppermute | solution.py:16
  180.6 532.7 %collective-permute-start.15 = (bf16[32,6,1,128]{3,0,2,1:T(8,128)(2,1)}, bf16[32,6,1,128]{3,0,2,1:T(8,128)(2,1)}, u32[]{:S(2)}, u32[]{:S(2)}) collective-permute-start(bf16[32,6,1,128]{3,0,2,1:T(8,128)(2,1)} %get-tuple-element.370), channel_id=1, source_target_pairs={{1,0},{2,1},{3,2},{5,4},{6,5},{7,6},{9,8},{10,9},{11,10},{13,12},{... | collective-permute-start | bytes 147464 | tf_op jit(solution)/shard_map/ppermute | solution.py:18
  737.4 381.8 %copy-start.57 = (bf16[32,1,8,128]{3,0,2,1:T(8,128)(2,1)S(1)}, bf16[32,1,8,128]{3,0,2,1:T(8,128)(2,1)}, u32[]{:S(2)}) copy-start(bf16[32,1,8,128]{3,0,2,1:T(8,128)(2,1)} %get-tuple-element.380) | copy-start | bytes 196612
  737.4 383.1 %copy-start.54 = (bf16[3,3,3,6,32]{4,3,2,1,0:T(8,128)(2,1)S(1)}, bf16[3,3,3,6,32]{4,3,2,1,0:T(8,128)(2,1)}, u32[]{:S(2)}) copy-start(bf16[3,3,3,6,32]{4,3,2,1,0:T(8,128)(2,1)} %reverse_bitcast_fusion.1) | copy-start | bytes 31108
  1117.9 3.4 collective-permute-start.16
  1119.2 5.5 collective-permute-start.17
  1124.8 9.9 collective-permute-start.18
  1130.7 6.9 collective-permute-start.19
  1148.6 54.1 %copy-start.1 = (bf16[16,4,128]{2,1,0:T(4,128)(2,1)S(1)}, bf16[16,4,128]{2,1,0:T(4,128)(2,1)}, u32[]{:S(2)}) copy-start(bf16[16,4,128]{2,1,0:T(4,128)(2,1)} %param.14) | copy-start | bytes 49156
  (59 other events, 536.1 us)
Sparse Core Ops, SparseCore 0:
  38.3 34.8 reduce-scatter.1
  164.3 548.9 all-reduce.16
  716.0 85.4 all-reduce.18
